TPU v7x, 32 devices: a whole 2x2x4 slice. The times are simulated.
32 devices in a mesh: atom: 4 (over y, x), pix: 8 (over z, core).
Axes of the slice: x: 2, y: 2, z: 4, core: 2. Of those that a mesh axis runs over, the one named last changes fastest.
Arguments:
- observed: float32 [224, 2048], P('atom', 'pix'), may hold values from -6 to 6
- library: float32 [224, 4096], P(None, ('atom', 'pix')), may hold values from -0.09375 to 0.09375
- image_split: float32 [224, 2048], P('atom', 'pix'), may hold values from -6 to 6
- image_dual: float32 [224, 2048], P('atom', 'pix'), may hold values from -4 to 4
- support: float32 [4096, 2048], P('atom', 'pix'), may hold values from -12 to 12
- support_dual: float32 [4096, 2048], P('atom', 'pix'), may hold values from -4 to 4
- positive: float32 [4096, 2048], P('atom', 'pix'), may hold values from 0 to 1
- positive_dual: float32 [4096, 2048], P('atom', 'pix'), may hold values from -4 to 4
Outputs:
- abundance: float32 [4096, 2048], P('atom', 'pix')
- image_split_next: float32 [224, 2048], P('atom', 'pix')
- image_dual_next: float32 [224, 2048], P('atom', 'pix')
- support_next: float32 [4096, 2048], P('atom', 'pix')
- support_dual_next: float32 [4096, 2048], P('atom', 'pix')
- positive_next: float32 [4096, 2048], P('atom', 'pix')
- positive_dual_next: float32 [4096, 2048], P('atom', 'pix')
All inputs are finite; a program needn't handle non-finite values.
Results may differ from a plain program's by a relative error of at most 0.0001.
Values sent between devices are 32-bit elements; how exact they have to be, the bound alone decides.
No kernel may reach another device: no remote copies, remote signals or barrier semaphores. Data moves between devices by JAX's collectives and lax.ppermute only.
A program may use at most 64 MiB of HBM per device.

v0:
```python
import math

import jax
import jax.numpy as jnp
from jax import lax
from jax.sharding import PartitionSpec as P

ITERS = 4


penalty = 0.5
shrink_rate = 0.4
epsilon = 1e-06


def matmul(left, right):
    return jnp.dot(left, right, precision=lax.Precision.HIGHEST, preferred_element_type=jnp.float32)


def on_device(
    observed, library, image_split, image_dual, support, support_dual, positive, positive_dual
):
    block = lax.all_gather(library, "pix", axis=1, tiled=True)
    bands = block.shape[0]
    gram = lax.psum(matmul(block, block.T), "atom")
    identity = jnp.eye(bands, dtype=jnp.float32)
    factor = jnp.linalg.cholesky(gram + 2.0 * identity)
    inverse = jax.scipy.linalg.cho_solve((factor, True), identity)
    own_bands = image_split.shape[0]
    pixels = observed.shape[1]
    first_band = lax.axis_index("atom") * own_bands
    gram_rows = lax.dynamic_slice_in_dim(gram, first_band, own_bands, 0)
    level = shrink_rate * math.sqrt(lax.axis_size("pix") * pixels)
    abundance = support
    for step in range(ITERS):
        combined = image_split + image_dual
        right = matmul(block.T, lax.all_gather(combined, "atom", axis=0, tiled=True))
        right = right + support + support_dual + positive + positive_dual
        partial_value = matmul(block, right)
        projected = lax.psum(partial_value, "atom")
        own_projected = lax.dynamic_slice_in_dim(projected, first_band, own_bands, 0)
        solved = matmul(inverse, projected)
        abundance = 0.5 * (right - matmul(block.T, solved))
        mixed = 0.5 * (own_projected - matmul(gram_rows, solved))
        image_split = (observed + penalty * (mixed - image_dual)) / (1.0 + penalty)
        image_dual = image_dual - (mixed - image_split)
        spread = abundance - support_dual
        squares = lax.psum(jnp.sum(spread * spread, axis=1), "pix")
        support = spread * jnp.maximum(1.0 - level / jnp.sqrt(squares + epsilon), 0.0)[:, None]
        support_dual = support_dual - (abundance - support)
        positive = jnp.maximum(abundance - positive_dual, 0.0)
        positive_dual = positive_dual - (abundance - positive)
    return (abundance, image_split, image_dual, support, support_dual, positive, positive_dual)


def solution(mesh):
    in_specs = (
        P("atom", "pix"),
        P(None, ("atom", "pix")),
        P("atom", "pix"),
        P("atom", "pix"),
        P("atom", "pix"),
        P("atom", "pix"),
        P("atom", "pix"),
        P("atom", "pix"),
    )
    out_specs = (
        P("atom", "pix"),
        P("atom", "pix"),
        P("atom", "pix"),
        P("atom", "pix"),
        P("atom", "pix"),
        P("atom", "pix"),
        P("atom", "pix"),
    )
    return jax.shard_map(
        on_device, mesh=mesh, in_specs=in_specs, out_specs=out_specs, check_vma=False
    )
```

profile of v0, /device:TPU:0, one launch (start us, length us, event | category | flops | bytes accessed | tf_op | source)
XLA Modules:
  0.0 446.5 jit_solution(3575130121402633482)
XLA Ops:
  8.1 10.5 %all_gather.15 = f32[224,256]{1,0:T(8,128)S(1)} all-gather(f32[56,256]{1,0:T(8,128)S(1)} %add.140), channel_id=1, replica_groups=mesh['atom'=4,'pix'=8] {'atom'}, dimensions={0}, use_global_device_ids=true | all-gather | bytes 286720 | tf_op jit(solution)/shard_map/all_gather | solution.py:37
  18.5 16.9 %all_gather.16 = f32[224,1024]{1,0:T(8,128)S(1)} all-gather(f32[224,128]{1,0:T(8,128)S(1)} %copy-done.36), channel_id=1, replica_groups=mesh['atom'=4,'pix'=8] {'pix'}, dimensions={1}, use_global_device_ids=true | all-gather | bytes 1032192 | tf_op jit(solution)/shard_map/all_gather | solution.py:23
  35.5 1.6 fusion.60
  37.4 1.9 copy.16
  39.4 2.9 copy.15
  42.3 2.5 copy.17
  44.8 2.7 fusion.17
  48.5 1.8 convolution_bitcast_fusion.11
  51.6 43.1 %all-reduce.15.cloned.1.call-done = (f32[224,256]{1,0:T(8,128)}, f32[224,224]{1,0:T(8,128)}) async-done(((f32[224,256]{1,0:T(8,128)}, f32[224,224]{1,0:T(8,128)}), (f32[224,256]{1,0:T(8,128)}, f32[224,224]{1,0:T(8,128)})) %all-reduce.15.cloned.1.call-update) | async-done | bytes 430096 | tf_op jit(solution)/shard_map/psum | solution.py:40
  98.3 13.2 %cholesky.50 = f32[128,128]{1,0:T(8,128)} custom-call(f32[128,128]{1,0:T(8,128)} %cholesky.121), custom_call_target="Cholesky" | custom-call | tf_op jit(solution)/shard_map/jit(cholesky)/cholesky | solution.py:27
  111.4 1.5 select_reduce_fusion
  113.6 11.3 %custom-call.18 = f32[1,128,128]{1,2,0:T(8,128)} custom-call(f32[1,128,128]{2,1,0:T(8,128)} %get-tuple-element.51), custom_call_target="InvertDiagBlocksLowerTriangular" | custom-call | tf_op jit(solution)/shard_map/jit(cholesky)/cholesky | solution.py:27
  126.8 1.6 convolution_subtract_fusion.6
  128.4 10.2 %cholesky.108 = f32[96,96]{1,0:T(8,128)} custom-call(f32[96,96]{1,0:T(8,128)} %convolution_subtract_fusion.6), custom_call_target="Cholesky" | custom-call | tf_op jit(solution)/shard_map/jit(cholesky)/cholesky | solution.py:27
  142.8 21.2 %custom-call.19 = f32[2,128,128]{1,2,0:T(8,128)} custom-call(f32[2,128,128]{2,1,0:T(8,128)} %pad_maximum_fusion.1), custom_call_target="InvertDiagBlocksLowerTriangular" | custom-call | tf_op jit(solution)/shard_map/jit(_cho_solve)/triangular_solve | solution.py:28
  167.0 1.8 convolution_subtract_fusion
  170.8 3.8 multiply_reduce_fusion.3
  175.4 9.4 %all_gather.17 = f32[224,256]{1,0:T(8,128)} all-gather(f32[56,256]{1,0:T(8,128)S(1)} %get-tuple-element.57), channel_id=1, replica_groups=mesh['atom'=4,'pix'=8] {'atom'}, dimensions={0}, use_global_device_ids=true | all-gather | bytes 286720 | tf_op jit(solution)/shard_map/all_gather | solution.py:37
  184.8 13.8 %psum.65 = f32[1024]{0:T(1024)S(1)} all-reduce(f32[1024]{0:T(1024)S(1)} %get-tuple-element.42), channel_id=1, replica_groups=mesh['atom'=4,'pix'=8] {'pix'}, use_global_device_ids=true, to_apply=%region_7.8 | all-reduce | flops 1024 | bytes 8192 | tf_op jit(solution)/shard_map/psum | solution.py:48
  198.7 2.3 subtract_subtract_fusion.7
  201.2 1.4 fusion.19
  203.5 1.8 convolution_bitcast_fusion.10
  205.4 40.2 %all-reduce.9.cloned.1.call-done = f32[224,256]{1,0:T(8,128)} async-done(((f32[224,256]{1,0:T(8,128)}), f32[224,256]{1,0:T(8,128)}) %all-reduce.9.cloned.1.call-update) | async-done | bytes 229392 | tf_op jit(solution)/shard_map/psum | solution.py:40
  245.6 1.5 fusion.34
  247.1 3.4 multiply_reduce_fusion.2
  250.6 1.7 fusion.50
  252.3 9.4 %all_gather.18 = f32[224,256]{1,0:T(8,128)} all-gather(f32[56,256]{1,0:T(8,128)S(1)} %get-tuple-element.59), channel_id=1, replica_groups=mesh['atom'=4,'pix'=8] {'atom'}, dimensions={0}, use_global_device_ids=true | all-gather | bytes 286720 | tf_op jit(solution)/shard_map/all_gather | solution.py:37
  261.7 14.0 %psum.67 = f32[1024]{0:T(1024)S(1)} all-reduce(f32[1024]{0:T(1024)S(1)} %get-tuple-element.40), channel_id=1, replica_groups=mesh['atom'=4,'pix'=8] {'pix'}, use_global_device_ids=true, to_apply=%region_10.11 | all-reduce | flops 1024 | bytes 8192 | tf_op jit(solution)/shard_map/psum | solution.py:48
  275.7 3.5 fusion.21
  280.2 1.8 convolution_bitcast_fusion.9
  282.0 40.2 %all-reduce.11.cloned.1.call-done = f32[224,256]{1,0:T(8,128)} async-done(((f32[224,256]{1,0:T(8,128)}), f32[224,256]{1,0:T(8,128)}) %all-reduce.11.cloned.1.call-update) | async-done | bytes 229392 | tf_op jit(solution)/shard_map/psum | solution.py:40
  322.2 1.5 fusion.33
  323.7 3.9 multiply_reduce_fusion.1
  327.6 15.9 %psum.69 = f32[1024]{0:T(1024)S(1)} all-reduce(f32[1024]{0:T(1024)S(1)} %get-tuple-element.62), channel_id=1, replica_groups=mesh['atom'=4,'pix'=8] {'pix'}, use_global_device_ids=true, to_apply=%region_13.14 | all-reduce | flops 1024 | bytes 8192 | tf_op jit(solution)/shard_map/psum | solution.py:48
  343.5 1.9 fusion.51
  345.4 8.8 %all_gather.19 = f32[224,256]{1,0:T(8,128)S(1)} all-gather(f32[56,256]{1,0:T(8,128)S(1)} %get-tuple-element.64), channel_id=1, replica_groups=mesh['atom'=4,'pix'=8] {'atom'}, dimensions={0}, use_global_device_ids=true | all-gather | bytes 286720 | tf_op jit(solution)/shard_map/all_gather | solution.py:37
  354.2 2.2 subtract_subtract_fusion.3
  357.0 1.8 fusion.23
  359.7 1.8 convolution_bitcast_fusion.8
  361.5 40.2 %all-reduce.13.cloned.1.call-done = f32[224,256]{1,0:T(8,128)} async-done(((f32[224,256]{1,0:T(8,128)}), f32[224,256]{1,0:T(8,128)}) %all-reduce.13.cloned.1.call-update) | async-done | bytes 229392 | tf_op jit(solution)/shard_map/psum | solution.py:40
  401.8 1.5 fusion.32
  403.3 4.1 multiply_reduce_fusion
  407.4 16.1 %psum.71 = f32[1024]{0:T(1024)S(1)} all-reduce(f32[1024]{0:T(1024)S(1)} %get-tuple-element.36), channel_id=1, replica_groups=mesh['atom'=4,'pix'=8] {'pix'}, use_global_device_ids=true, to_apply=%region_16.17 | all-reduce | flops 1024 | bytes 8192 | tf_op jit(solution)/shard_map/psum | solution.py:48
  423.6 2.6 copy.25
  426.2 5.1 %subtract_subtract_fusion = (f32[1024,256]{0,1:T(8,128)}, f32[1024,256]{0,1:T(8,128)}, f32[1024,256]{0,1:T(8,128)}, f32[1024,256]{0,1:T(8,128)}) fusion(f32[1024,256]{0,1:T(8,128)} %get-tuple-element.66, f32[1024,256]{0,1:T(8,128)} %get-tuple-element.63, f32[1024,256]{0,1:T(8,128)S(1)} %get-tuple-element.61, f32[1024,256]{0,1:T(8,128)S(1)} %copy-done.2, ...), kind=kLoop, calls=%fused_computation.47 | loop fusion | flops 4980736 | bytes 11538432 | tf_op jit(solution)/shard_map/sub | solution.py:52
  431.3 2.6 copy.29
  436.6 1.3 copy.27
  438.0 1.7 subtract_subtract_fusion.8
  (116 shorter events, 24.6 us)
Async XLA Ops:
  7.2 87.5 %all-reduce.15.cloned.1.call-start = ((), (), s32[]{:S(2)}) async-start(), calls=%async_computation.3 | async-start | bytes 917504 | tf_op jit(solution)/shard_map/psum | solution.py:40
  8.1 10.5 %copy-start.36 = (f32[224,128]{1,0:T(8,128)S(1)}, f32[224,128]{1,0:T(8,128)}, u32[]{:S(2)}) copy-start(f32[224,128]{1,0:T(8,128)} %param.9) | copy-start | bytes 344068
  35.5 1.6 copy-start.22
  37.4 163.6 %copy-start = (f32[1024,256]{0,1:T(8,128)}, f32[1024,256]{0,1:T(8,128)S(1)}, u32[]{:S(2)}) copy-start(f32[1024,256]{0,1:T(8,128)S(1)} %copy.18) | copy-start | bytes 3145732
  39.4 131.4 %copy-start.6 = (f32[1024,256]{0,1:T(8,128)}, f32[1024,256]{0,1:T(8,128)S(1)}, u32[]{:S(2)}) copy-start(f32[1024,256]{0,1:T(8,128)S(1)} %copy.16) | copy-start | bytes 3145732
  47.6 1.0 copy-start.10
  50.4 195.2 %all-reduce.9.cloned.1.call-start = ((), (), s32[]{:S(2)}) async-start(), calls=%async_computation | async-start | bytes 458752 | tf_op jit(solution)/shard_map/psum | solution.py:40
  95.7 0.9 copy-start.17
  97.6 16.0 %copy-start.30 = (f32[224,224]{1,0:T(8,128)}, f32[224,224]{1,0:T(8,128)S(1)}, u32[]{:S(2)}) copy-start(f32[224,224]{1,0:T(8,128)S(1)} %fusion.28) | copy-start | bytes 602116
  124.8 0.9 copy-start.37
  141.4 0.7 copy-start.29
  142.2 21.9 %copy-start.35 = (pred[224,224]{1,0:T(32,128)(4,1)S(1)}, pred[224,224]{1,0:T(32,128)(4,1)}, u32[]{:S(2)}) copy-start(pred[224,224]{1,0:T(32,128)(4,1)} %iota_compare_fusion) | copy-start | bytes 150532
  165.2 1.2 copy-start.32
  168.9 1.3 copy-start.33
  170.7 3.8 copy-start.21
  170.7 3.8 copy-start.23
  198.7 2.3 copy-start.3
  198.7 2.5 copy-start.11
  198.7 2.5 copy-start.28
  202.6 1.0 copy-start.12
  205.4 116.9 %all-reduce.11.cloned.1.call-start = ((), (), s32[]{:S(2)}) async-start(), calls=%async_computation.1 | async-start | bytes 458752 | tf_op jit(solution)/shard_map/psum | solution.py:40
  247.1 3.5 copy-start.24
  247.1 3.5 copy-start.26
  279.2 1.0 copy-start.9
  282.0 119.8 %all-reduce.13.cloned.1.call-start = ((), (), s32[]{:S(2)}) async-start(), calls=%async_computation.2 | async-start | bytes 458752 | tf_op jit(solution)/shard_map/psum | solution.py:40
  323.7 3.9 copy-start.20
  354.2 2.2 copy-start.1
  354.2 2.2 copy-start.4
  354.2 2.5 copy-start.5
  354.2 2.8 copy-start.7
  357.0 1.8 copy-start.8
  358.8 1.0 copy-start.13
  403.3 4.2 copy-start.18
  423.6 2.6 copy-start.2
  431.3 2.6 copy-start.16
  434.0 1.3 copy-start.15
  435.3 1.3 copy-start.14
  436.6 1.3 copy-start.19
  436.6 1.3 copy-start.25
  436.6 1.3 copy-start.27
  436.6 1.3 copy-start.31
  436.6 1.3 copy-start.34
Sparse Core Ops, SparseCore 0:
  50.5 44.1 all-reduce.14
  205.5 40.0 all-reduce.8
  282.1 40.0 all-reduce.10
  361.7 40.0 all-reduce.12
where the time goes:
time: 452 us; the launch traced here: 446 us
  waiting for transfers between devices  164 us (36%)
  blocking collectives  115 us (25%)
  other arithmetic  73.3 us (16%)
  matrix products  53.1 us (12%)
  local copies, waits for them, and re-layouts  24.9 us (6%)
  between operations  15.9 us (4%)
    psum x4, waiting for transfers between devices, on_device(): projected = lax.psum(partial_value, 'atom')  164 us
    psum x4, blocking collectives, on_device(): squares = lax.psum(jnp.sum(spread * spread, axis=1), 'pix')  59.8 us
    dot_general x21, matrix products, matmul(): jnp.dot(left, right, precision=lax.Precision.HIGHEST, preferred_element_t...  44.6 us
    another operation x7, other arithmetic, on_device(): factor = jnp.linalg.cholesky(gram + 2.0 * identity)  38.2 us
    all_gather x4, blocking collectives, on_device(): lax.all_gather(combined, 'atom', axis=0, tiled=True)  38.1 us
    unnamed x85, local copies, waits for them, and re-layouts  22.4 us
    another operation x6, other arithmetic, on_device(): inverse = jax.scipy.linalg.cho_solve((factor, True), identity)  22 us
    all_gather x1, blocking collectives, on_device(): block = lax.all_gather(library, 'pix', axis=1, tiled=True)  16.9 us
  transfers between devices with their start and end apart: 4, of which 4 were waited for; matrix products, arithmetic and copies ran while one was open for 0% of the time, Pallas kernels for 0%

commit v1 on v0

v1 whole, which is shorter than its diff:
```python
import functools
import math

import jax
import jax.numpy as jnp
from jax import lax
from jax.experimental import pallas as pl
from jax.experimental.pallas import tpu as pltpu
from jax.sharding import PartitionSpec as P

ITERS = 4

penalty = 0.5
shrink_rate = 0.4
epsilon = 1e-06
LANES = 128
NEWTON_CAP = 40
VMEM_LIMIT = 20 * 1024 * 1024

f32 = jnp.float32
bf16 = jnp.bfloat16
EXACT = lax.Precision.HIGHEST


def split(value):
    high = value.astype(bf16)
    return high, (value - high.astype(f32)).astype(bf16)


def dot(left, right, dims=((1,), (0,)), precision=None):
    return lax.dot_general(
        left, right, (dims, ((), ())), precision=precision, preferred_element_type=f32
    )


def dot3(left, right):
    (lh, ll), (rh, rl) = left, right
    return dot(lh, rh) + (dot(lh, rl) + dot(ll, rh))


def call(body, outs, scratch=(), name=None):
    return pl.pallas_call(
        body,
        out_shape=outs,
        scratch_shapes=list(scratch),
        compiler_params=pltpu.CompilerParams(vmem_limit_bytes=VMEM_LIMIT),
        name=name,
    )


def shape(*dims, dtype=f32):
    return jax.ShapeDtypeStruct(dims, dtype)


def packed_rows(bands):
    return bands if bands <= LANES else bands + (bands - LANES)


def gram_body(block_ref, packed_ref):
    bands = block_ref.shape[0]
    block = block_ref[...]
    gram = dot(block, block, ((1,), (1,)), EXACT)
    if bands <= LANES:
        packed_ref[...] = gram
        return
    packed_ref[:bands, :] = gram[:, :LANES]
    packed_ref[bands:, :] = jnp.zeros((bands - LANES, LANES), f32)
    packed_ref[bands:, : bands - LANES] = gram[LANES:, LANES:]


def transpose_body(block_ref, high_ref, low_ref):
    bands, atoms = block_ref.shape
    for first in range(0, atoms, LANES):
        high, low = split(block_ref[:, first : first + LANES].T)
        high_ref[first : first + LANES, :] = high
        low_ref[first : first + LANES, :] = low


def start_body(
    own_first, block_ref, image_ref, dual_ref, a_ref, b_ref, c_ref, d_ref, sum_ref, right_ref
):
    own = image_ref.shape[0]

    @pl.when(pl.program_id(0) == 0)
    def _():
        right_ref[...] = jnp.zeros_like(right_ref)
        first = pl.multiple_of(own_first[0], 8)
        right_ref[pl.ds(first, own), :] = 2.0 * (image_ref[...] + dual_ref[...])

    total = (a_ref[...] + b_ref[...]) + (c_ref[...] + d_ref[...])
    sum_ref[...] = total
    right_ref[...] -= dot(block_ref[...], total, precision=EXACT)


def start(own_first, block, image, dual, a, b, c, d):
    bands, atoms = block.shape
    own, pixels = image.shape
    rows = min(atoms, 256)
    wide = pl.BlockSpec((rows, pixels), lambda i, _: (i, 0))
    whole = pl.BlockSpec((own, pixels), lambda i, _: (0, 0))
    return pl.pallas_call(
        start_body,
        out_shape=(shape(atoms, pixels), shape(bands, pixels)),
        grid_spec=pltpu.PrefetchScalarGridSpec(
            num_scalar_prefetch=1,
            grid=(atoms // rows,),
            in_specs=[pl.BlockSpec((bands, rows), lambda i, _: (0, i)), whole, whole]
            + [wide] * 4,
            out_specs=(wide, pl.BlockSpec((bands, pixels), lambda i, _: (0, 0))),
        ),
        compiler_params=pltpu.CompilerParams(
            vmem_limit_bytes=VMEM_LIMIT, dimension_semantics=("arbitrary",)
        ),
        name="start",
    )(own_first, block, image, dual, a, b, c, d)


def inverse_body(one_ref, two_ref, inverse_ref, matrix_ref, residual_ref):
    bands = inverse_ref.shape[0]
    rows = lax.broadcasted_iota(jnp.int32, (bands, bands), 0)
    columns = lax.broadcasted_iota(jnp.int32, (bands, bands), 1)
    identity = jnp.where(rows == columns, 1.0, 0.0).astype(f32)
    packed = one_ref[...] + two_ref[...]
    if bands <= LANES:
        matrix_ref[...] = packed
    else:
        rest = bands - LANES
        matrix_ref[:, :LANES] = packed[:bands]
        matrix_ref[:LANES, LANES:] = packed[LANES:bands].T
        matrix_ref[LANES:, LANES:] = packed[bands:, :rest]
    matrix = matrix_ref[...] + 2.0 * identity
    matrix_ref[...] = matrix
    bound = jnp.max(jnp.sum(jnp.abs(matrix), axis=0))
    first = 2.0 / (2.0 + bound)
    residual = identity - first * matrix
    inverse_ref[...] = first * (identity + residual)

    def measure():
        residual_ref[...] = identity - dot(matrix_ref[...], inverse_ref[...], precision=EXACT)
        return jnp.max(jnp.sum(jnp.abs(residual_ref[...]), axis=0))

    def unfinished(state):
        step, size = state
        return jnp.logical_and(step < NEWTON_CAP, size > 1e-3)

    def improve():
        held = inverse_ref[...]
        inverse_ref[...] = held + dot(held, residual_ref[...], precision=EXACT)

    def again(state):
        step, _ = state
        improve()
        return step + 1, measure()

    lax.while_loop(unfinished, again, (jnp.int32(0), measure()))
    improve()


def factor_body(own_first, inverse_ref, block_ref, th_ref, tl_ref, eh_ref, el_ref):
    own = eh_ref.shape[1]
    inverse = inverse_ref[...]
    halves = split(inverse)
    atoms = block_ref.shape[1]
    step = min(atoms, 256)
    for first in range(0, atoms, step):
        high, low = split(dot3(halves, split(block_ref[:, first : first + step])))
        th_ref[:, first : first + step] = high
        tl_ref[:, first : first + step] = low
    mine = inverse_ref[pl.ds(pl.multiple_of(own_first[0], 8), own), :]
    high, low = split(2.0 * mine.T)
    eh_ref[...] = high
    el_ref[...] = low


def row_sums(squared, out_ref, index):
    pixels = squared.shape[1]
    folded = squared[:, :LANES]
    for first in range(LANES, pixels, LANES):
        folded = folded + squared[:, first : first + LANES]
    out_ref[index : index + 1, :] = jnp.sum(folded.T, axis=0, keepdims=True)


def image_step(own_first, u_ref, observed_ref, image_ref, dual_ref, image_out, dual_out):
    own = image_ref.shape[0]
    u = u_ref[pl.ds(pl.multiple_of(own_first[0], 8), own), :]
    image = image_ref[...]
    new = (2.0 * observed_ref[...] + image - u) / 3.0
    image_out[...] = new
    dual_out[...] = new - image + u


def first_body(
    own_first, one, two, inverse, lth, ltl, total, support_dual, positive_dual,
    observed, image, dual, spread, q, squares, image_out, dual_out, u_ref,
):
    u_ref[...] = dot(inverse[...], one[...] + two[...], precision=EXACT)
    halves = split(u_ref[...])
    atoms = spread.shape[0]
    for index in range(atoms // LANES):
        rows = slice(index * LANES, (index + 1) * LANES)
        y = dot3((lth[rows, :], ltl[rows, :]), halves)
        x = 0.5 * (total[rows, :] + y)
        new = x - support_dual[rows, :]
        spread[rows, :] = new
        q[rows, :] = x - positive_dual[rows, :]
        row_sums(new * new, squares, index)
    image_step(own_first, u_ref, observed, image, dual, image_out, dual_out)


def middle_body(
    own_first, one, two, lth, ltl, spread, q, w, observed, image, dual,
    spread_out, q_out, squares, image_out, dual_out, u_ref,
):
    u_ref[...] = one[...] + two[...]
    halves = split(u_ref[...])
    atoms = spread.shape[0]
    for index in range(atoms // LANES):
        rows = slice(index * LANES, (index + 1) * LANES)
        y = dot3((lth[rows, :], ltl[rows, :]), halves)
        old = q[rows, :]
        new = 0.5 * (spread[rows, :] + jnp.abs(old) + y)
        spread_out[rows, :] = new
        q_out[rows, :] = 0.5 * (w[rows, :] + old + y)
        row_sums(new * new, squares, index)
    image_step(own_first, u_ref, observed, image, dual, image_out, dual_out)


def last_body(
    own_first, one, two, lth, ltl, spread, q, w, observed, image, dual,
    spread_out, x_out, positive_out, positive_dual_out, squares, image_out, dual_out, u_ref,
):
    u_ref[...] = one[...] + two[...]
    halves = split(u_ref[...])
    atoms = spread.shape[0]
    for index in range(atoms // LANES):
        rows = slice(index * LANES, (index + 1) * LANES)
        y = dot3((lth[rows, :], ltl[rows, :]), halves)
        old = q[rows, :]
        new = 0.5 * (spread[rows, :] + jnp.abs(old) + y)
        spread_out[rows, :] = new
        row_sums(new * new, squares, index)
        newer = 0.5 * (w[rows, :] + old + y)
        x_out[rows, :] = newer + jnp.maximum(-old, 0.0)
        positive_out[rows, :] = jnp.maximum(newer, 0.0)
        positive_dual_out[rows, :] = jnp.maximum(-newer, 0.0)
    image_step(own_first, u_ref, observed, image, dual, image_out, dual_out)


def shrink_of(parts, level):
    squares = jnp.sum(parts[...], axis=0)
    return jnp.maximum(1.0 - level / jnp.sqrt(squares + epsilon), 0.0)


def column(row, pixels):
    turned = jnp.broadcast_to(row, (LANES, LANES)).T
    return jnp.concatenate([turned] * (pixels // LANES), axis=1)


def shrink_body(level, parts, spread, q, th, tl, eh, el, image, dual, w, right, hh, hl):
    gain = 2.0 * shrink_of(parts, level) - 1.0
    atoms, pixels = spread.shape
    for index in range(atoms // LANES):
        rows = slice(index * LANES, (index + 1) * LANES)
        scaled = column(gain[index : index + 1, :], pixels) * spread[rows, :]
        w[rows, :] = scaled
        high, low = split(scaled + jnp.abs(q[rows, :]))
        hh[rows, :] = high
        hl[rows, :] = low
    combined = split(image[...] + dual[...])
    right[...] = dot3((eh[...], el[...]), combined) - dot3(
        (th[...], tl[...]), (hh[...], hl[...])
    )


def end_body(level, parts, spread, support_out, dual_out):
    shrink = shrink_of(parts, level)
    atoms, pixels = spread.shape
    for index in range(atoms // LANES):
        rows = slice(index * LANES, (index + 1) * LANES)
        held = spread[rows, :]
        support = column(shrink[index : index + 1, :], pixels) * held
        support_out[rows, :] = support
        dual_out[rows, :] = support - held


def over_atoms(value):
    size = lax.axis_size("atom")
    if size == 1 or size & (size - 1):
        return lax.psum(value, "atom"), jnp.zeros_like(value)
    step = 1
    while True:
        other = lax.ppermute(value, "atom", [(i, i ^ step) for i in range(size)])
        step *= 2
        if step == size:
            return value, other
        value = value + other


def over_pixels(value):
    size = lax.axis_size("pix")
    copies = jnp.broadcast_to(value[None], (size,) + value.shape)
    return lax.all_to_all(copies, "pix", 0, 0, tiled=True)


def on_device(
    observed, library, image_split, image_dual, support, support_dual, positive, positive_dual
):
    block = lax.all_gather(library, "pix", axis=1, tiled=True)
    bands, atoms = block.shape
    own, pixels = image_split.shape
    level = shrink_rate * math.sqrt(lax.axis_size("pix") * pixels)
    own_first = (lax.axis_index("atom") * own).astype(jnp.int32).reshape(1)

    smem = pl.BlockSpec(memory_space=pltpu.SMEM)
    vmem = pl.BlockSpec(memory_space=pltpu.VMEM)

    def placed(body, outs, count, scratch, name):
        return pl.pallas_call(
            body,
            out_shape=outs,
            in_specs=[smem] + [vmem] * (count - 1),
            out_specs=tuple(vmem for _ in outs),
            scratch_shapes=list(scratch),
            compiler_params=pltpu.CompilerParams(vmem_limit_bytes=VMEM_LIMIT),
            name=name,
        )

    packed = call(gram_body, shape(packed_rows(bands), min(bands, LANES)), name="gram")(block)
    gram_one, gram_two = over_atoms(packed)
    total, right = start(
        own_first, block, image_split, image_dual, support, support_dual, positive, positive_dual
    )
    right_one, right_two = over_atoms(right)
    half = shape(atoms, bands, dtype=bf16)
    lth, ltl = call(transpose_body, (half, half), name="turn")(block)
    inverse = call(
        inverse_body,
        shape(bands, bands),
        [pltpu.VMEM((bands, bands), f32), pltpu.VMEM((bands, bands), f32)],
        name="inverse",
    )(gram_one, gram_two)
    half = shape(bands, atoms, dtype=bf16)
    edge = shape(bands, own, dtype=bf16)
    th, tl, eh, el = placed(factor_body, (half, half, edge, edge), 3, (), "factor")(
        own_first, inverse, block
    )

    wide = shape(atoms, pixels)
    band = shape(own, pixels)
    sums = shape(atoms // LANES, LANES)
    u_scratch = pltpu.VMEM((bands, pixels), f32)
    spread, q, squares, image, dual = placed(
        first_body, (wide, wide, sums, band, band), 12, [u_scratch], "first"
    )(
        own_first, right_one, right_two, inverse, lth, ltl, total, support_dual, positive_dual,
        observed, image_split, image_dual,
    )
    for step in range(1, ITERS):
        w, right = call(
            functools.partial(shrink_body, level),
            (wide, shape(bands, pixels)),
            [pltpu.VMEM((atoms, pixels), bf16), pltpu.VMEM((atoms, pixels), bf16)],
            name="shrink",
        )(over_pixels(squares), spread, q, th, tl, eh, el, image, dual)
        one, two = over_atoms(right)
        operands = (own_first, one, two, lth, ltl, spread, q, w, observed, image, dual)
        if step < ITERS - 1:
            spread, q, squares, image, dual = placed(
                middle_body, (wide, wide, sums, band, band), 11, [u_scratch], "middle"
            )(*operands)
        else:
            spread, x, pos, pos_dual, squares, image, dual = placed(
                last_body, (wide, wide, wide, wide, sums, band, band), 11, [u_scratch], "last"
            )(*operands)
    new_support, new_support_dual = call(
        functools.partial(end_body, level), (wide, wide), name="end"
    )(over_pixels(squares), spread)
    return (x, image, dual, new_support, new_support_dual, pos, pos_dual)


def solution(mesh):
    wide = P("atom", "pix")
    in_specs = (wide, P(None, ("atom", "pix"))) + (wide,) * 6
    return jax.shard_map(
        on_device, mesh=mesh, in_specs=in_specs, out_specs=(wide,) * 7, check_vma=False
    )
```

time: 452 us -> 145 us (0.32); the launches traced: 446 us -> 145 us
  waiting for transfers between devices: 164 us -> 46 us
  other arithmetic: 73.3 us -> 0.15 us
  blocking collectives: 115 us -> 43.3 us
  matrix products: 53.1 us -> 0 us
  starting transfers between devices: 0.69 us -> 19.8 us
  Pallas kernels: 0 us -> 18.2 us
  between operations: 15.9 us -> 0.92 us
  local copies, waits for them, and re-layouts: 24.9 us -> 16.3 us
    psum x4 -> x0, waiting for transfers between devices: 164 us -> none  [on_device(): projected = lax.psum(partial_value, 'atom')]
    another operation x13 -> x0, other arithmetic: 60.3 us -> none  [the longest x7 38.2 us: on_device(): factor = jnp.linalg.cholesky(gram + 2.0 * identity)]
    psum x4 -> x0, blocking collectives: 59.8 us -> none  [on_device(): squares = lax.psum(jnp.sum(spread * spread, axis=1), 'pix')]
    dot_general x21 -> x0, matrix products: 44.6 us -> none  [matmul(): jnp.dot(left, right, precision=lax.Precision.HIGHEST, preferred_element_t...]
    ppermute x0 -> x10, waiting for transfers between devices: none -> 43.7 us  [over_atoms(): other = lax.ppermute(value, 'atom', [(i, i ^ step) for i in range(size)])]
    all_gather x4 -> x0, blocking collectives: 38.1 us -> none  [on_device(): lax.all_gather(combined, 'atom', axis=0, tiled=True)]
    all_to_all x0 -> x3, blocking collectives: none -> 25.3 us  [over_pixels(): return lax.all_to_all(copies, 'pix', 0, 0, tiled=True)]
    pallas_call x0 -> x13, Pallas kernels: none -> 18.2 us  [the longest x1 4.62 us: on_device(): call(inverse_body, shape(bands, bands), [pltpu.VMEM((bands, bands), f32),...]
  transfers between devices with their start and end apart: 4 -> 11, of which waited for: 4 -> 10; matrix products, arithmetic and copies ran while one was open for 0% -> 0% of each run, Pallas kernels for 0% -> 4%
where the time goes in v1:
time: 145 us
  waiting for transfers between devices  46 us (32%)
  blocking collectives  43.3 us (30%)
  starting transfers between devices  19.8 us (14%)
  Pallas kernels  18.2 us (13%)
  local copies, waits for them, and re-layouts  16.3 us (11%)
    ppermute x10, waiting for transfers between devices, over_atoms(): other = lax.ppermute(value, 'atom', [(i, i ^ step) for i in range(size)])  43.7 us
    all_to_all x3, blocking collectives, over_pixels(): return lax.all_to_all(copies, 'pix', 0, 0, tiled=True)  25.3 us
    all_gather x1, blocking collectives, on_device(): block = lax.all_gather(library, 'pix', axis=1, tiled=True)  18 us
    unnamed x58, local copies, waits for them, and re-layouts  15.6 us
    ppermute x10, starting transfers between devices, over_atoms(): other = lax.ppermute(value, 'atom', [(i, i ^ step) for i in range(size)])  14.8 us
    all_to_all x1, starting transfers between devices, over_pixels(): return lax.all_to_all(copies, 'pix', 0, 0, tiled=True)  5.01 us
    pallas_call x1, Pallas kernels, on_device(): call(inverse_body, shape(bands, bands), [pltpu.VMEM((bands, bands), f32),...  4.62 us
    pallas_call x3, Pallas kernels, on_device(): call(functools.partial(shrink_body, level), (wide, shape(bands, pixels)),...  3.12 us
  transfers between devices with their start and end apart: 11, of which 10 were waited for; matrix products, arithmetic and copies ran while one was open for 0% of the time, Pallas kernels for 4%

profile of v1, /device:TPU:0, one launch (start us, length us, event | category | flops | bytes accessed | tf_op | source)
XLA Modules:
  0.0 144.5 jit_solution(2704004291863075275)
XLA Ops:
  0.7 18.0 %all_gather.3.block_ref = f32[224,1024]{1,0:T(8,128)S(1)} all-gather(f32[224,128]{1,0:T(8,128)} %param.9), channel_id=1, replica_groups=mesh['atom'=4,'pix'=8] {'pix'}, dimensions={1}, use_global_device_ids=true | all-gather | bytes 1032192 | tf_op jit(solution)/shard_map/all_gather | solution.py:308
  18.6 1.2 copy-done.3
  19.9 1.2 copy-done.5
  21.1 1.2 copy-done.11
  22.3 1.2 copy-done.12
  23.5 1.7 %start.1 = (f32[1024,256]{1,0:T(8,128)S(1)}, f32[224,256]{1,0:T(8,128)S(1)}) custom-call(s32[1]{0:T(128)} %bitcast.own_first, f32[224,1024]{1,0:T(8,128)S(1)} %all_gather.3.block_ref, f32[56,256]{1,0:T(8,128)S(1)} %copy-done.26, f32[56,256]{1,0:T(8,128)S(1)} %copy-done.27, f32[1024,256]{1,0:T(8,128)S(1)} %copy-done.11, f32[1024,256]{1,0:T(8,128)S(1)} %copy-done.3, ...), custom_call_target="tpu_custom_call" | custom-call | tf_op jit(solution)/shard_map/start/pallas_call | solution.py:101
  25.2 1.6 %collective-permute-start = (f32[224,256]{1,0:T(8,128)S(1)}, f32[224,256]{1,0:T(8,128)S(1)}, u32[]{:S(2)}, u32[]{:S(2)}) collective-permute-start(f32[224,256]{1,0:T(8,128)S(1)} %get-tuple-element.45), channel_id=1, source_target_pairs={{0,8},{8,0},{16,24},{24,16},{1,9},{9,1},{17,25},{25,17},{2,10},{10... | collective-permute-start | bytes 688136 | tf_op jit(solution)/shard_map/ppermute | solution.py:292
  26.8 0.9 gram.1
  28.3 5.5 %collective-permute-done = f32[224,256]{1,0:T(8,128)S(1)} collective-permute-done((f32[224,256]{1,0:T(8,128)S(1)}, f32[224,256]{1,0:T(8,128)S(1)}, u32[]{:S(2)}, u32[]{:S(2)}) %collective-permute-start) | collective-permute-done | bytes 229408 | tf_op jit(solution)/shard_map/ppermute | solution.py:292
  33.8 1.6 %collective-permute-start.1 = (f32[224,256]{1,0:T(8,128)S(1)}, f32[224,256]{1,0:T(8,128)S(1)}, u32[]{:S(2)}, u32[]{:S(2)}) collective-permute-start(f32[224,256]{1,0:T(8,128)S(1)} %add.15.one), channel_id=1, source_target_pairs={{0,16},{8,24},{16,0},{24,8},{1,17},{9,25},{17,1},{25,9},{2,18},{10... | collective-permute-start | bytes 688136 | tf_op jit(solution)/shard_map/ppermute | solution.py:292
  35.4 1.3 collective-permute-done.2
  36.7 1.6 %collective-permute-start.3 = (f32[320,128]{1,0:T(8,128)S(1)}, f32[320,128]{1,0:T(8,128)S(1)}, u32[]{:S(2)}, u32[]{:S(2)}) collective-permute-start(f32[320,128]{1,0:T(8,128)S(1)} %add.16.one_ref), channel_id=1, source_target_pairs={{0,16},{8,24},{16,0},{24,8},{1,17},{9,25},{17,1},{25,9},{2,18},{10... | collective-permute-start | bytes 491528 | tf_op jit(solution)/shard_map/ppermute | solution.py:292
  38.6 5.1 %collective-permute-done.3.two_ref = f32[320,128]{1,0:T(8,128)S(1)} collective-permute-done((f32[320,128]{1,0:T(8,128)S(1)}, f32[320,128]{1,0:T(8,128)S(1)}, u32[]{:S(2)}, u32[]{:S(2)}) %collective-permute-start.3) | collective-permute-done | bytes 163872 | tf_op jit(solution)/shard_map/ppermute | solution.py:292
  43.8 4.6 %inverse.1.inverse_ref = f32[224,224]{1,0:T(8,128)S(1)} custom-call(f32[320,128]{1,0:T(8,128)S(1)} %add.16.one_ref, f32[320,128]{1,0:T(8,128)S(1)} %collective-permute-done.3.two_ref), custom_call_target="tpu_custom_call" | custom-call | tf_op jit(solution)/shard_map/inverse/pallas_call | solution.py:336
  48.4 1.4 first.1
  49.8 1.0 copy-done
  52.6 5.0 %all-to-all-start = ((f32[8,8,128]{2,1,0:T(8,128)}), f32[8,8,128]{2,1,0:T(8,128)}, u32[]{:S(2)}, u32[]{:S(2)}) async-start(f32[8,8,128]{2,1,0:T(8,128)} %broadcast_in_dim.8), calls=%async_computation | async-start | bytes 65536 | tf_op jit(solution)/shard_map/all_to_all | solution.py:302
  57.7 0.9 copy-done.10
  59.2 0.8 copy-done.7
  61.2 2.3 %all-to-all-done.parts = f32[8,8,128]{2,1,0:T(8,128)} async-done(((f32[8,8,128]{2,1,0:T(8,128)}), f32[8,8,128]{2,1,0:T(8,128)}, u32[]{:S(2)}, u32[]{:S(2)}) %all-to-all-start) | async-done | bytes 32800 | tf_op jit(solution)/shard_map/all_to_all | solution.py:302
  63.5 1.2 copy-done.1
  64.7 1.0 copy-done.8
  65.8 0.8 copy-done.15
  66.6 0.8 copy-done.18
  67.4 0.8 copy-done.21
  68.2 0.8 copy-done.24
  69.0 1.6 %shrink.3 = (f32[1024,256]{1,0:T(8,128)S(1)}, f32[224,256]{1,0:T(8,128)S(1)}) custom-call(f32[8,8,128]{2,1,0:T(8,128)} %all-to-all-done.parts, f32[1024,256]{1,0:T(8,128)S(1)} %get-tuple-element.50.spread, f32[1024,256]{1,0:T(8,128)S(1)} %copy-done.1, bf16[224,1024]{1,0:T(8,128)(2,1)S(1)} %get-tuple-element.52.th, bf16[224,1024]{1,0:T(8,128)(2,1)S(1)} %copy-done.8, ...), custom_call_target="tpu_custom_call" | custom-call | tf_op jit(solution)/shard_map/shrink/pallas_call | solution.py:359
  70.7 1.6 %collective-permute-start.4 = (f32[224,256]{1,0:T(8,128)S(1)}, f32[224,256]{1,0:T(8,128)S(1)}, u32[]{:S(2)}, u32[]{:S(2)}) collective-permute-start(f32[224,256]{1,0:T(8,128)S(1)} %get-tuple-element.58), channel_id=1, source_target_pairs={{0,8},{8,0},{16,24},{24,16},{1,9},{9,1},{17,25},{25,17},{2,10},{10... | collective-permute-start | bytes 688136 | tf_op jit(solution)/shard_map/ppermute | solution.py:292
  72.2 5.8 %collective-permute-done.4 = f32[224,256]{1,0:T(8,128)S(1)} collective-permute-done((f32[224,256]{1,0:T(8,128)S(1)}, f32[224,256]{1,0:T(8,128)S(1)}, u32[]{:S(2)}, u32[]{:S(2)}) %collective-permute-start.4) | collective-permute-done | bytes 229408 | tf_op jit(solution)/shard_map/ppermute | solution.py:292
  78.0 1.6 %collective-permute-start.5 = (f32[224,256]{1,0:T(8,128)S(1)}, f32[224,256]{1,0:T(8,128)S(1)}, u32[]{:S(2)}, u32[]{:S(2)}) collective-permute-start(f32[224,256]{1,0:T(8,128)S(1)} %add.17.one), channel_id=1, source_target_pairs={{0,16},{8,24},{16,0},{24,8},{1,17},{9,25},{17,1},{25,9},{2,18},{10... | collective-permute-start | bytes 688136 | tf_op jit(solution)/shard_map/ppermute | solution.py:292
  79.6 4.9 %collective-permute-done.5.two = f32[224,256]{1,0:T(8,128)S(1)} collective-permute-done((f32[224,256]{1,0:T(8,128)S(1)}, f32[224,256]{1,0:T(8,128)S(1)}, u32[]{:S(2)}, u32[]{:S(2)}) %collective-permute-start.5) | collective-permute-done | bytes 229408 | tf_op jit(solution)/shard_map/ppermute | solution.py:292
  84.5 0.8 middle.2
  85.3 9.1 %all_to_all.20.parts = f32[8,8,128]{2,1,0:T(8,128)S(1)} all-to-all(f32[8,8,128]{2,1,0:T(8,128)S(1)} %broadcast_in_dim.9), channel_id=1, replica_groups=mesh['atom'=4,'pix'=8] {'pix'}, dimensions={0} | all-to-all | bytes 65536 | tf_op jit(solution)/shard_map/all_to_all | solution.py:302
  94.4 0.8 shrink.4
  95.2 1.6 %collective-permute-start.6 = (f32[224,256]{1,0:T(8,128)S(1)}, f32[224,256]{1,0:T(8,128)S(1)}, u32[]{:S(2)}, u32[]{:S(2)}) collective-permute-start(f32[224,256]{1,0:T(8,128)S(1)} %get-tuple-element.65), channel_id=1, source_target_pairs={{0,8},{8,0},{16,24},{24,16},{1,9},{9,1},{17,25},{25,17},{2,10},{10... | collective-permute-start | bytes 688136 | tf_op jit(solution)/shard_map/ppermute | solution.py:292
  96.7 5.7 %collective-permute-done.6 = f32[224,256]{1,0:T(8,128)S(1)} collective-permute-done((f32[224,256]{1,0:T(8,128)S(1)}, f32[224,256]{1,0:T(8,128)S(1)}, u32[]{:S(2)}, u32[]{:S(2)}) %collective-permute-start.6) | collective-permute-done | bytes 229408 | tf_op jit(solution)/shard_map/ppermute | solution.py:292
  102.5 1.6 %collective-permute-start.7 = (f32[224,256]{1,0:T(8,128)S(1)}, f32[224,256]{1,0:T(8,128)S(1)}, u32[]{:S(2)}, u32[]{:S(2)}) collective-permute-start(f32[224,256]{1,0:T(8,128)S(1)} %add.18.one), channel_id=1, source_target_pairs={{0,16},{8,24},{16,0},{24,8},{1,17},{9,25},{17,1},{25,9},{2,18},{10... | collective-permute-start | bytes 688136 | tf_op jit(solution)/shard_map/ppermute | solution.py:292
  104.1 4.9 %collective-permute-done.7.two = f32[224,256]{1,0:T(8,128)S(1)} collective-permute-done((f32[224,256]{1,0:T(8,128)S(1)}, f32[224,256]{1,0:T(8,128)S(1)}, u32[]{:S(2)}, u32[]{:S(2)}) %collective-permute-start.7) | collective-permute-done | bytes 229408 | tf_op jit(solution)/shard_map/ppermute | solution.py:292
  109.0 0.8 middle.3
  109.7 8.1 %all_to_all.21.parts = f32[8,8,128]{2,1,0:T(8,128)S(1)} all-to-all(f32[8,8,128]{2,1,0:T(8,128)S(1)} %broadcast_in_dim.10), channel_id=1, replica_groups=mesh['atom'=4,'pix'=8] {'pix'}, dimensions={0} | all-to-all | bytes 65536 | tf_op jit(solution)/shard_map/all_to_all | solution.py:302
  117.9 0.8 shrink.5
  118.6 1.6 %collective-permute-start.8 = (f32[224,256]{1,0:T(8,128)S(1)}, f32[224,256]{1,0:T(8,128)S(1)}, u32[]{:S(2)}, u32[]{:S(2)}) collective-permute-start(f32[224,256]{1,0:T(8,128)S(1)} %get-tuple-element.72), channel_id=1, source_target_pairs={{0,8},{8,0},{16,24},{24,16},{1,9},{9,1},{17,25},{25,17},{2,10},{10... | collective-permute-start | bytes 688136 | tf_op jit(solution)/shard_map/ppermute | solution.py:292
  120.2 5.7 %collective-permute-done.8 = f32[224,256]{1,0:T(8,128)S(1)} collective-permute-done((f32[224,256]{1,0:T(8,128)S(1)}, f32[224,256]{1,0:T(8,128)S(1)}, u32[]{:S(2)}, u32[]{:S(2)}) %collective-permute-start.8) | collective-permute-done | bytes 229408 | tf_op jit(solution)/shard_map/ppermute | solution.py:292
  126.0 1.6 %collective-permute-start.9 = (f32[224,256]{1,0:T(8,128)S(1)}, f32[224,256]{1,0:T(8,128)S(1)}, u32[]{:S(2)}, u32[]{:S(2)}) collective-permute-start(f32[224,256]{1,0:T(8,128)S(1)} %add.19.one), channel_id=1, source_target_pairs={{0,16},{8,24},{16,0},{24,8},{1,17},{9,25},{17,1},{25,9},{2,18},{10... | collective-permute-start | bytes 688136 | tf_op jit(solution)/shard_map/ppermute | solution.py:292
  127.5 4.9 %collective-permute-done.9.two = f32[224,256]{1,0:T(8,128)S(1)} collective-permute-done((f32[224,256]{1,0:T(8,128)S(1)}, f32[224,256]{1,0:T(8,128)S(1)}, u32[]{:S(2)}, u32[]{:S(2)}) %collective-permute-start.9) | collective-permute-done | bytes 229408 | tf_op jit(solution)/shard_map/ppermute | solution.py:292
  132.4 2.5 %last.1 = (f32[1024,256]{1,0:T(8,128)S(1)}, f32[1024,256]{1,0:T(8,128)}, f32[1024,256]{1,0:T(8,128)}, f32[1024,256]{1,0:T(8,128)}, f32[8,128]{1,0:T(8,128)S(1)}, /*index=5*/f32[56,256]{1,0:T(8,128)}, f32[56,256]{1,0:T(8,128)}) custom-call(s32[1]{0:T(128)} %bitcast.own_first, f32[224,256]{1,0:T(8,128)S(1)} %add.19.one, ...), custom_call_target="tpu_custom_call" | custom-call | tf_op jit(solution)/shard_map/last/pallas_call | solution.py:372
  134.9 8.1 %all_to_all.22.parts = f32[8,8,128]{2,1,0:T(8,128)S(1)} all-to-all(f32[8,8,128]{2,1,0:T(8,128)S(1)} %broadcast_in_dim.11), channel_id=1, replica_groups=mesh['atom'=4,'pix'=8] {'pix'}, dimensions={0} | all-to-all | bytes 65536 | tf_op jit(solution)/shard_map/all_to_all | solution.py:302
  143.0 1.5 %end.1 = (f32[1024,256]{1,0:T(8,128)}, f32[1024,256]{1,0:T(8,128)}) custom-call(f32[8,8,128]{2,1,0:T(8,128)S(1)} %all_to_all.22.parts, f32[1024,256]{1,0:T(8,128)S(1)} %get-tuple-element.78.spread), custom_call_target="tpu_custom_call" | custom-call | tf_op jit(solution)/shard_map/end/pallas_call | solution.py:375
  (58 shorter events, 4.9 us)
Async XLA Ops:
  0.6 18.0 %copy-start.26 = (f32[56,256]{1,0:T(8,128)S(1)}, f32[56,256]{1,0:T(8,128)}, u32[]{:S(2)}) copy-start(f32[56,256]{1,0:T(8,128)} %image.1) | copy-start | bytes 172036
  0.6 18.0 %copy-start.27 = (f32[56,256]{1,0:T(8,128)S(1)}, f32[56,256]{1,0:T(8,128)}, u32[]{:S(2)}) copy-start(f32[56,256]{1,0:T(8,128)} %dual.1) | copy-start | bytes 172036
  18.6 1.2 copy-start.3
  19.9 1.2 copy-start.5
  21.1 1.2 copy-start.11
  22.3 1.2 copy-start.12
  25.2 8.5 %collective-permute-start = (f32[224,256]{1,0:T(8,128)S(1)}, f32[224,256]{1,0:T(8,128)S(1)}, u32[]{:S(2)}, u32[]{:S(2)}) collective-permute-start(f32[224,256]{1,0:T(8,128)S(1)} %get-tuple-element.45), channel_id=1, source_target_pairs={{0,8},{8,0},{16,24},{24,16},{1,9},{9,1},{17,25},{25,17},{2,10},{10... | collective-permute-start | bytes 688136 | tf_op jit(solution)/shard_map/ppermute | solution.py:292
  27.7 8.9 %collective-permute-start.2 = (f32[320,128]{1,0:T(8,128)S(1)}, f32[320,128]{1,0:T(8,128)S(1)}, u32[]{:S(2)}, u32[]{:S(2)}) collective-permute-start(f32[320,128]{1,0:T(8,128)S(1)} %gram.1), channel_id=1, source_target_pairs={{0,8},{8,0},{16,24},{24,16},{1,9},{9,1},{17,25},{25,17},{2,10},{10... | collective-permute-start | bytes 491528 | tf_op jit(solution)/shard_map/ppermute | solution.py:292
  33.8 14.6 %copy-start.6 = (f32[1024,256]{1,0:T(8,128)S(1)}, f32[1024,256]{1,0:T(8,128)}, u32[]{:S(2)}) copy-start(f32[1024,256]{1,0:T(8,128)} %positive_dual.1) | copy-start | bytes 3145732
  33.8 14.6 %copy-start.4 = (f32[1024,256]{1,0:T(8,128)S(1)}, f32[1024,256]{1,0:T(8,128)}, u32[]{:S(2)}) copy-start(f32[1024,256]{1,0:T(8,128)} %support_dual.1) | copy-start | bytes 3145732
  33.8 14.6 %collective-permute-start.1 = (f32[224,256]{1,0:T(8,128)S(1)}, f32[224,256]{1,0:T(8,128)S(1)}, u32[]{:S(2)}, u32[]{:S(2)}) collective-permute-start(f32[224,256]{1,0:T(8,128)S(1)} %add.15.one), channel_id=1, source_target_pairs={{0,16},{8,24},{16,0},{24,8},{1,17},{9,25},{17,1},{25,9},{2,18},{10... | collective-permute-start | bytes 688136 | tf_op jit(solution)/shard_map/ppermute | solution.py:292
  36.7 7.1 %collective-permute-start.3 = (f32[320,128]{1,0:T(8,128)S(1)}, f32[320,128]{1,0:T(8,128)S(1)}, u32[]{:S(2)}, u32[]{:S(2)}) collective-permute-start(f32[320,128]{1,0:T(8,128)S(1)} %add.16.one_ref), channel_id=1, source_target_pairs={{0,16},{8,24},{16,0},{24,8},{1,17},{9,25},{17,1},{25,9},{2,18},{10... | collective-permute-start | bytes 491528 | tf_op jit(solution)/shard_map/ppermute | solution.py:292
  38.6 9.8 %copy-start.13 = (f32[56,256]{1,0:T(8,128)S(1)}, f32[56,256]{1,0:T(8,128)}, u32[]{:S(2)}) copy-start(f32[56,256]{1,0:T(8,128)} %observed.7) | copy-start | bytes 172036
  38.6 9.8 %copy-start.28 = (f32[56,256]{1,0:T(8,128)S(1)}, f32[56,256]{1,0:T(8,128)}, u32[]{:S(2)}) copy-start(f32[56,256]{1,0:T(8,128)} %dual.1) | copy-start | bytes 172036
  48.4 1.4 copy-start.9
  49.8 1.0 copy-start
  50.8 0.6 copy-start.20
  51.4 0.6 copy-start.23
  52.6 10.9 %all-to-all-start = ((f32[8,8,128]{2,1,0:T(8,128)}), f32[8,8,128]{2,1,0:T(8,128)}, u32[]{:S(2)}, u32[]{:S(2)}) async-start(f32[8,8,128]{2,1,0:T(8,128)} %broadcast_in_dim.8), calls=%async_computation | async-start | bytes 65536 | tf_op jit(solution)/shard_map/all_to_all | solution.py:302
  57.7 0.9 copy-start.10
  59.2 0.8 copy-start.7
  59.9 0.6 copy-start.14
  60.6 0.6 copy-start.17
  63.5 1.2 copy-start.1
  64.7 1.0 copy-start.8
  65.8 0.8 copy-start.15
  66.6 0.8 copy-start.18
  67.4 0.8 copy-start.21
  68.2 0.8 copy-start.24
  69.0 15.4 %copy-start.2 = (f32[1024,256]{1,0:T(8,128)S(1)}, f32[1024,256]{1,0:T(8,128)}, u32[]{:S(2)}) copy-start(f32[1024,256]{1,0:T(8,128)} %copy-done) | copy-start | bytes 3145732
  70.6 13.8 %copy-start.22 = (f32[56,256]{1,0:T(8,128)S(1)}, f32[56,256]{1,0:T(8,128)}, u32[]{:S(2)}) copy-start(f32[56,256]{1,0:T(8,128)} %copy-done.20) | copy-start | bytes 172036
  70.7 13.8 %copy-start.25 = (f32[56,256]{1,0:T(8,128)S(1)}, f32[56,256]{1,0:T(8,128)}, u32[]{:S(2)}) copy-start(f32[56,256]{1,0:T(8,128)} %copy-done.23) | copy-start | bytes 172036
  70.7 7.3 %collective-permute-start.4 = (f32[224,256]{1,0:T(8,128)S(1)}, f32[224,256]{1,0:T(8,128)S(1)}, u32[]{:S(2)}, u32[]{:S(2)}) collective-permute-start(f32[224,256]{1,0:T(8,128)S(1)} %get-tuple-element.58), channel_id=1, source_target_pairs={{0,8},{8,0},{16,24},{24,16},{1,9},{9,1},{17,25},{25,17},{2,10},{10... | collective-permute-start | bytes 688136 | tf_op jit(solution)/shard_map/ppermute | solution.py:292
  78.0 6.4 %collective-permute-start.5 = (f32[224,256]{1,0:T(8,128)S(1)}, f32[224,256]{1,0:T(8,128)S(1)}, u32[]{:S(2)}, u32[]{:S(2)}) collective-permute-start(f32[224,256]{1,0:T(8,128)S(1)} %add.17.one), channel_id=1, source_target_pairs={{0,16},{8,24},{16,0},{24,8},{1,17},{9,25},{17,1},{25,9},{2,18},{10... | collective-permute-start | bytes 688136 | tf_op jit(solution)/shard_map/ppermute | solution.py:292
  84.5 9.9 %copy-start.19 = (bf16[224,56]{1,0:T(8,128)(2,1)S(1)}, bf16[224,56]{1,0:T(8,128)(2,1)}, u32[]{:S(2)}) copy-start(bf16[224,56]{1,0:T(8,128)(2,1)} %copy-done.17) | copy-start | bytes 75268
  85.3 9.1 %copy-start.16 = (bf16[224,56]{1,0:T(8,128)(2,1)S(1)}, bf16[224,56]{1,0:T(8,128)(2,1)}, u32[]{:S(2)}) copy-start(bf16[224,56]{1,0:T(8,128)(2,1)} %copy-done.14) | copy-start | bytes 75268
  95.2 7.3 %collective-permute-start.6 = (f32[224,256]{1,0:T(8,128)S(1)}, f32[224,256]{1,0:T(8,128)S(1)}, u32[]{:S(2)}, u32[]{:S(2)}) collective-permute-start(f32[224,256]{1,0:T(8,128)S(1)} %get-tuple-element.65), channel_id=1, source_target_pairs={{0,8},{8,0},{16,24},{24,16},{1,9},{9,1},{17,25},{25,17},{2,10},{10... | collective-permute-start | bytes 688136 | tf_op jit(solution)/shard_map/ppermute | solution.py:292
  102.5 6.4 %collective-permute-start.7 = (f32[224,256]{1,0:T(8,128)S(1)}, f32[224,256]{1,0:T(8,128)S(1)}, u32[]{:S(2)}, u32[]{:S(2)}) collective-permute-start(f32[224,256]{1,0:T(8,128)S(1)} %add.18.one), channel_id=1, source_target_pairs={{0,16},{8,24},{16,0},{24,8},{1,17},{9,25},{17,1},{25,9},{2,18},{10... | collective-permute-start | bytes 688136 | tf_op jit(solution)/shard_map/ppermute | solution.py:292
  118.6 7.3 %collective-permute-start.8 = (f32[224,256]{1,0:T(8,128)S(1)}, f32[224,256]{1,0:T(8,128)S(1)}, u32[]{:S(2)}, u32[]{:S(2)}) collective-permute-start(f32[224,256]{1,0:T(8,128)S(1)} %get-tuple-element.72), channel_id=1, source_target_pairs={{0,8},{8,0},{16,24},{24,16},{1,9},{9,1},{17,25},{25,17},{2,10},{10... | collective-permute-start | bytes 688136 | tf_op jit(solution)/shard_map/ppermute | solution.py:292
  126.0 6.4 %collective-permute-start.9 = (f32[224,256]{1,0:T(8,128)S(1)}, f32[224,256]{1,0:T(8,128)S(1)}, u32[]{:S(2)}, u32[]{:S(2)}) collective-permute-start(f32[224,256]{1,0:T(8,128)S(1)} %add.19.one), channel_id=1, source_target_pairs={{0,16},{8,24},{16,0},{24,8},{1,17},{9,25},{17,1},{25,9},{2,18},{10... | collective-permute-start | bytes 688136 | tf_op jit(solution)/shard_map/ppermute | solution.py:292
